TPU v7x, 32 devices: a whole 2x2x4 slice. The times are simulated.
32 devices in a mesh: section: 2 (over core), ctx: 4 (over y, x), tp: 4 (over z).
Axes of the slice: x: 2, y: 2, z: 4, core: 2. Of those that a mesh axis runs over, the one named last changes fastest.
Arguments:
- inputs: bfloat16 [4, 1024, 2048], P(None, ('ctx', 'tp')), may hold values from -6 to 6
- segments: int32 [4, 1024], replicated, may hold values from 0 to 3, never falling along the last dimension, each value on 1 to 512 neighbouring positions
- cotangent: bfloat16 [4, 1024, 2048], P(None, ('ctx', 'tp')), may hold values from -6 to 6
- ln_gain: bfloat16 [2, 2048], P('section'), may hold values from 0.5 to 1.5
- ln_bias: bfloat16 [2, 2048], P('section'), may hold values from -3 to 3
- qkv_weight: bfloat16 [2, 3, 2048, 2048], P('section', None, None, 'tp'), may hold values from -1 to 1, as said below
- qkv_bias: bfloat16 [2, 3, 2048], P('section', None, 'tp'), may hold values from -3 to 3
- dense_weight: bfloat16 [2, 2048, 2048], P('section', 'tp'), may hold values from -0.75 to 0.75
- fc1_weight: bfloat16 [2, 2048, 8192], P('section', None, 'tp'), may hold values from -0.125 to 0.125
- fc1_bias: bfloat16 [2, 8192], P('section', 'tp'), may hold values from -3 to 3
- fc2_weight: bfloat16 [2, 8192, 2048], P('section', 'tp'), may hold values from -0.0625 to 0.0625
- out_bias: bfloat16 [2, 2048], P('section'), may hold values from -3 to 3
Outputs:
- layer_outputs: bfloat16 [2, 4, 1024, 2048], P('section', None, ('ctx', 'tp'))
- input_grads: bfloat16 [2, 4, 1024, 2048], P('section', None, ('ctx', 'tp'))
- ln_gain_grad: float32 [2, 2048], P('section')
- ln_bias_grad: float32 [2, 2048], P('section')
- qkv_weight_grad: float32 [2, 3, 2048, 2048], P('section', None, None, 'tp')
- qkv_bias_grad: float32 [2, 3, 2048], P('section', None, 'tp')
- dense_weight_grad: float32 [2, 2048, 2048], P('section', 'tp')
- fc1_weight_grad: float32 [2, 2048, 8192], P('section', None, 'tp')
- fc1_bias_grad: float32 [2, 8192], P('section', 'tp')
- fc2_weight_grad: float32 [2, 8192, 2048], P('section', 'tp')
- out_bias_grad: float32 [2, 2048], P('section')
Inputs may be any that keep to these rules, and one draw needn't show every extreme that they name: `segments`: within a sequence the ids never fall; each of the 4 documents has 1 to 512 tokens, one exactly 512. `qkv_weight`: entries of order 2048^(-1/2).
All inputs are finite; a program needn't handle non-finite values.
Results may differ from a plain program's by a relative error of at most 0.02.
Values may be sent and summed in bfloat16 or wider, within the bound.
No kernel may reach another device: no remote copies, remote signals or barrier semaphores. Data moves between devices by JAX's collectives and lax.ppermute only.
A program may use at most 640 MiB of HBM per device.

v0:
```python
import jax
import jax.numpy as jnp
from jax import lax
from jax.sharding import PartitionSpec as P

HEAD = 64
ROT = 32
EPSILON = 1e-05
NEGATIVE = -1e30
GELU_ROOT = 0.7978845608028654
GELU_CUBE = 0.044715


def from_behind(x, axis, by):
    length = lax.axis_size(axis)
    pairs = [(i, i + by) for i in range(length) if 0 <= i + by < length]
    return lax.ppermute(x, axis, pairs)


def rope_tables(positions, rot_dims):
    half_dims = rot_dims // 2
    frequency = 10000.0 ** (-(2.0 * jnp.arange(half_dims, dtype=jnp.float32)) / rot_dims)
    angles = positions.astype(jnp.float32)[:, None] * frequency[None, :]
    return (jnp.cos(angles)[:, None, :], jnp.sin(angles)[:, None, :])


def rotate(values_in, cosine, sine, rot_dims):
    half_dims = rot_dims // 2
    lower_half = values_in[..., :half_dims]
    upper_half = values_in[..., half_dims:rot_dims]
    return jnp.concatenate(
        [
            lower_half * cosine - upper_half * sine,
            upper_half * cosine + lower_half * sine,
            values_in[..., rot_dims:],
        ],
        axis=-1,
    )


def unrotate(grads_in, cosine, sine, rot_dims):
    half_dims = rot_dims // 2
    lower_half = grads_in[..., :half_dims]
    upper_half = grads_in[..., half_dims:rot_dims]
    return jnp.concatenate(
        [
            lower_half * cosine + upper_half * sine,
            upper_half * cosine - lower_half * sine,
            grads_in[..., rot_dims:],
        ],
        axis=-1,
    )


def gelu_slope(pre_act):
    tangent = jnp.tanh(GELU_ROOT * (pre_act + GELU_CUBE * pre_act * pre_act * pre_act))
    return 0.5 * (1.0 + tangent) + 0.5 * pre_act * (1.0 - tangent * tangent) * GELU_ROOT * (
        1.0 + 3.0 * GELU_CUBE * pre_act * pre_act
    )


def normalize(x_rows):
    centered = x_rows - jnp.mean(x_rows, axis=1, keepdims=True)
    inv_std = lax.rsqrt(jnp.mean(centered * centered, axis=1, keepdims=True) + EPSILON)
    return (centered * inv_std, inv_std)


def take_slot(buffer, slot_index):
    return lax.dynamic_index_in_dim(buffer, slot_index, 0, keepdims=False)


def put_slot(buffer, slot_index, leaf_value, active):
    return lax.dynamic_update_index_in_dim(
        buffer, jnp.where(active, leaf_value, take_slot(buffer, slot_index)), slot_index, 0
    )


def on_device(
    inputs,
    segments,
    cotangent,
    ln_gain,
    ln_bias,
    qkv_weight,
    qkv_bias,
    dense_weight,
    fc1_weight,
    fc1_bias,
    fc2_weight,
    out_bias,
):
    sections = lax.axis_size("section")
    section_id = lax.axis_index("section")
    ctx_id = lax.axis_index("ctx")
    batches, row_count, model_width = inputs.shape
    ctx_rows = row_count * lax.axis_size("tp")
    total_rows = ctx_rows * lax.axis_size("ctx")
    local_dim = qkv_weight.shape[3]
    heads_local = local_dim // HEAD
    score_scale = HEAD ** (-0.5)
    gain_vec = ln_gain[0].astype(jnp.float32)
    shift_vec = ln_bias[0].astype(jnp.float32)
    w_in = jnp.concatenate(
        [qkv_weight[0, 0], qkv_weight[0, 1], qkv_weight[0, 2], fc1_weight[0]], axis=1
    )
    bias_in = jnp.concatenate([qkv_bias[0].reshape(-1), fc1_bias[0]]).astype(jnp.float32)
    w_out = jnp.concatenate([dense_weight[0], fc2_weight[0]], axis=0)
    bias_vec = out_bias[0].astype(jnp.float32)
    query_pos = ctx_id * ctx_rows + jnp.arange(ctx_rows, dtype=jnp.int32)
    cosine, sine = rope_tables(query_pos, ROT)
    key_pos = jnp.arange(total_rows, dtype=jnp.int32)
    contract_rows = (((0,), (0,)), ((), ()))
    contract_cols = (((1,), (1,)), ((), ()))
    received = jnp.zeros((row_count, model_width), jnp.bfloat16)
    layer_out = jnp.zeros((batches, row_count, model_width), jnp.bfloat16)
    buffers = None
    for clock_tick in range(batches + sections - 1):
        micro_batch = clock_tick - section_id
        active = (micro_batch >= 0) & (micro_batch < batches)
        slot_index = jnp.clip(micro_batch, 0, batches - 1)
        x_rows = jnp.where(section_id == 0, take_slot(inputs, slot_index), received).astype(
            jnp.float32
        )
        doc_all = take_slot(segments, slot_index)
        normalized, inv_std = normalize(x_rows)
        normed_b = (normalized * gain_vec + shift_vec).astype(jnp.bfloat16)
        doc_rows = lax.dynamic_slice_in_dim(doc_all, ctx_id * ctx_rows, ctx_rows)
        stored = {}
        projected = jnp.dot(
            lax.all_gather(normed_b, "tp", axis=0, tiled=True),
            w_in,
            preferred_element_type=jnp.float32,
        )
        projected = projected + bias_in
        query_pre = projected[:, :local_dim].reshape(ctx_rows, heads_local, HEAD)
        key_pre = projected[:, local_dim : 2 * local_dim].reshape(ctx_rows, heads_local, HEAD)
        queries_b = rotate(query_pre, cosine, sine, ROT).astype(jnp.bfloat16)
        keys_b = rotate(key_pre, cosine, sine, ROT).astype(jnp.bfloat16)
        values_b = (
            projected[:, 2 * local_dim : 3 * local_dim]
            .reshape(ctx_rows, heads_local, HEAD)
            .astype(jnp.bfloat16)
        )
        up_pre = projected[:, 3 * local_dim :]
        run_max = jnp.full((heads_local, ctx_rows), NEGATIVE, jnp.float32)
        keys_part = lax.all_gather(keys_b, "ctx", axis=0, tiled=True)
        values_part = lax.all_gather(values_b, "ctx", axis=0, tiled=True)
        part_rows = keys_part.shape[0]
        part_pos = jnp.arange(part_rows, dtype=jnp.int32)
        allowed = (part_pos[None, :] <= query_pos[:, None]) & (
            doc_all[None, :] == doc_rows[:, None]
        )
        scores = (
            jnp.einsum("qhd,khd->hqk", queries_b, keys_part, preferred_element_type=jnp.float32)
            * score_scale
        )
        scores = jnp.where(allowed[None], scores, NEGATIVE)
        new_max = jnp.maximum(run_max, jnp.max(scores, axis=2))
        weights = jnp.where(allowed[None], jnp.exp(scores - new_max[:, :, None]), 0.0)
        run_sum = jnp.sum(weights, axis=2)
        accumulated = jnp.einsum(
            "hqk,khd->hqd",
            weights.astype(jnp.bfloat16),
            values_part,
            preferred_element_type=jnp.float32,
        )
        run_max, run_sum, accumulated = (new_max, run_sum, accumulated)
        attended = jnp.transpose(accumulated / run_sum[:, :, None], (1, 0, 2))
        log_total = run_max + jnp.log(run_sum)
        attended_b = attended.reshape(ctx_rows, local_dim).astype(jnp.bfloat16)
        gelu_b = jax.nn.gelu(up_pre, approximate=True).astype(jnp.bfloat16)
        branch_in = jnp.concatenate([attended_b, gelu_b], axis=1)
        branch = lax.psum_scatter(
            jnp.dot(branch_in, w_out, preferred_element_type=jnp.float32).astype(jnp.bfloat16),
            "tp",
            scatter_dimension=0,
            tiled=True,
        ).astype(jnp.float32)
        result = x_rows + branch + bias_vec
        stored["x_rows"] = x_rows.astype(jnp.bfloat16)
        stored["queries"] = queries_b
        stored["keys"] = keys_b
        stored["values"] = values_b
        stored["up_pre"] = up_pre
        stored["branch_in"] = branch_in
        stored["attended"] = attended
        stored["log_total"] = log_total
        result, stored = (result, stored)
        result_b = result.astype(jnp.bfloat16)
        if buffers is None:
            buffers = jax.tree.map(
                lambda leaf_value: jnp.zeros((batches,) + leaf_value.shape, leaf_value.dtype),
                stored,
            )
        buffers = jax.tree.map(
            lambda buffer, leaf_value: put_slot(buffer, slot_index, leaf_value, active),
            buffers,
            stored,
        )
        layer_out = put_slot(layer_out, slot_index, result_b, active)
        received = from_behind(result_b, "section", 1)
    received = jnp.zeros((row_count, model_width), jnp.bfloat16)
    grad_inputs = jnp.zeros((batches, row_count, model_width), jnp.bfloat16)
    totals = None
    for clock_tick in range(batches + sections - 1):
        micro_batch = clock_tick - (sections - 1 - section_id)
        active = (micro_batch >= 0) & (micro_batch < batches)
        slot_index = jnp.clip(micro_batch, 0, batches - 1)
        grad_out = jnp.where(
            section_id == sections - 1, take_slot(cotangent, slot_index), received
        ).astype(jnp.float32)
        stored = jax.tree.map(lambda buffer: take_slot(buffer, slot_index), buffers)
        doc_all = take_slot(segments, slot_index)
        backward_normalized, backward_inv_std = normalize(stored["x_rows"].astype(jnp.float32))
        backward_normed_b = (backward_normalized * gain_vec + shift_vec).astype(jnp.bfloat16)
        backward_doc_rows = lax.dynamic_slice_in_dim(doc_all, ctx_id * ctx_rows, ctx_rows)
        backward_branch_in = stored["branch_in"]
        grad_out_b = grad_out.astype(jnp.bfloat16)
        fold_pieces = lax.all_gather(grad_out_b, "tp", axis=0, tiled=True)
        grad_w = lax.dot_general(
            backward_branch_in, fold_pieces, contract_rows, preferred_element_type=jnp.float32
        )
        grad_rows = lax.dot_general(
            fold_pieces, w_out, contract_cols, preferred_element_type=jnp.float32
        )
        grad_attn_b = (
            grad_rows[:, :local_dim].astype(jnp.bfloat16).reshape(ctx_rows, heads_local, HEAD)
        )
        grad_up = grad_rows[:, local_dim:] * gelu_slope(stored["up_pre"])
        row_delta = jnp.transpose(
            jnp.sum(grad_attn_b.astype(jnp.float32) * stored["attended"], axis=2)
        )
        keys_all = lax.all_gather(stored["keys"], "ctx", axis=0, tiled=True)
        values_all = lax.all_gather(stored["values"], "ctx", axis=0, tiled=True)
        backward_queries_b = stored["queries"]
        backward_allowed = (key_pos[None, :] <= query_pos[:, None]) & (
            doc_all[None, :] == backward_doc_rows[:, None]
        )
        backward_scores = (
            jnp.einsum(
                "qhd,khd->hqk", backward_queries_b, keys_all, preferred_element_type=jnp.float32
            )
            * score_scale
        )
        probs = jnp.where(
            backward_allowed[None], jnp.exp(backward_scores - stored["log_total"][:, :, None]), 0.0
        )
        grad_probs = jnp.einsum(
            "qhd,khd->hqk", grad_attn_b, values_all, preferred_element_type=jnp.float32
        )
        grad_scores_b = (probs * (grad_probs - row_delta[:, :, None])).astype(jnp.bfloat16)
        grad_query = (
            jnp.einsum("hqk,khd->qhd", grad_scores_b, keys_all, preferred_element_type=jnp.float32)
            * score_scale
        )
        probs_b = probs.astype(jnp.bfloat16)
        grad_key_part = (
            jnp.einsum(
                "hqk,qhd->khd",
                grad_scores_b,
                backward_queries_b,
                preferred_element_type=jnp.float32,
            )
            * score_scale
        )
        grad_value_part = jnp.einsum(
            "hqk,qhd->khd", probs_b, grad_attn_b, preferred_element_type=jnp.float32
        )
        key_grads = (
            lax.psum_scatter(
                jnp.concatenate([grad_key_part, grad_value_part], axis=2)
                .reshape(ctx_rows * lax.axis_size("ctx"), 2 * local_dim)
                .astype(jnp.bfloat16),
                "ctx",
                scatter_dimension=0,
                tiled=True,
            )
            .astype(jnp.float32)
            .reshape(ctx_rows, heads_local, 2 * HEAD)
        )
        grad_key_raw = key_grads[..., :HEAD]
        grad_value = key_grads[..., HEAD:]
        grad_key = unrotate(grad_key_raw, cosine, sine, ROT)
        grad_query = unrotate(grad_query, cosine, sine, ROT)
        grad_proj_b = jnp.concatenate(
            [
                grad_query.reshape(ctx_rows, local_dim),
                grad_key.reshape(ctx_rows, local_dim),
                grad_value.reshape(ctx_rows, local_dim),
                grad_up,
            ],
            axis=1,
        ).astype(jnp.bfloat16)
        grad_bias_in = jnp.sum(grad_proj_b.astype(jnp.float32), axis=0)
        grad_w_in = lax.dot_general(
            lax.all_gather(backward_normed_b, "tp", axis=0, tiled=True),
            grad_proj_b,
            contract_rows,
            preferred_element_type=jnp.float32,
        )
        grad_normed = lax.psum_scatter(
            lax.dot_general(
                grad_proj_b, w_in, contract_cols, preferred_element_type=jnp.float32
            ).astype(jnp.bfloat16),
            "tp",
            scatter_dimension=0,
            tiled=True,
        ).astype(jnp.float32)
        grad_gain = jnp.sum(grad_normed * backward_normalized, axis=0)
        grad_shift = jnp.sum(grad_normed, axis=0)
        scaled = grad_normed * gain_vec
        grad_x = grad_out + backward_inv_std * (
            scaled
            - jnp.mean(scaled, axis=1, keepdims=True)
            - backward_normalized * jnp.mean(scaled * backward_normalized, axis=1, keepdims=True)
        )
        grad_x, terms = (
            grad_x,
            (grad_w_in, grad_w, grad_bias_in, grad_gain, grad_shift, jnp.sum(grad_out, axis=0)),
        )
        terms = tuple((jnp.where(active, term_value, 0.0) for term_value in terms))
        totals = terms if totals is None else jax.tree.map(jnp.add, totals, terms)
        grad_x_b = grad_x.astype(jnp.bfloat16)
        grad_inputs = put_slot(grad_inputs, slot_index, grad_x_b, active)
        received = from_behind(grad_x_b, "section", -1)
    total_w_in, total_w_out, total_bias_in, total_gain, total_shift, total_bias_out = totals
    sum_w_in, sum_w_out, sum_bias_in, sum_gain, sum_shift, sum_bias_out = (
        lax.psum(total_w_in.astype(jnp.bfloat16), "ctx").astype(jnp.float32),
        lax.psum(total_w_out.astype(jnp.bfloat16), "ctx").astype(jnp.float32),
        lax.psum(total_bias_in.astype(jnp.bfloat16), "ctx").astype(jnp.float32),
        lax.psum(total_gain.astype(jnp.bfloat16), "ctx").astype(jnp.float32),
        lax.psum(total_shift.astype(jnp.bfloat16), "ctx").astype(jnp.float32),
        lax.psum(total_bias_out.astype(jnp.bfloat16), "ctx").astype(jnp.float32),
    )
    sum_gain, sum_shift, sum_bias_out = lax.psum((sum_gain, sum_shift, sum_bias_out), "tp")
    qkv_grad = jnp.transpose(
        sum_w_in[:, : 3 * local_dim].reshape(model_width, 3, local_dim), (1, 0, 2)
    )
    return (
        layer_out[None],
        grad_inputs[None],
        sum_gain[None],
        sum_shift[None],
        qkv_grad[None],
        sum_bias_in[: 3 * local_dim].reshape(3, local_dim)[None],
        sum_w_out[:local_dim][None],
        sum_w_in[:, 3 * local_dim :][None],
        sum_bias_in[3 * local_dim :][None],
        sum_w_out[local_dim:][None],
        sum_bias_out[None],
    )


def solution(mesh):
    return jax.shard_map(
        on_device,
        mesh=mesh,
        in_specs=(
            P(None, ("ctx", "tp"), None),
            P(),
            P(None, ("ctx", "tp"), None),
            P("section", None),
            P("section", None),
            P("section", None, None, "tp"),
            P("section", None, "tp"),
            P("section", "tp", None),
            P("section", None, "tp"),
            P("section", "tp"),
            P("section", "tp", None),
            P("section", None),
        ),
        out_specs=(
            P("section", None, ("ctx", "tp"), None),
            P("section", None, ("ctx", "tp"), None),
            P("section", None),
            P("section", None),
            P("section", None, None, "tp"),
            P("section", None, "tp"),
            P("section", "tp", None),
            P("section", None, "tp"),
            P("section", "tp"),
            P("section", "tp", None),
            P("section", None),
        ),
        check_vma=False,
    )
```

profile of v0, /device:TPU:0, one launch (start us, length us, event | category | flops | bytes accessed | tf_op | source)
XLA Modules:
  0.0 2298.0 jit_solution(12967685389564836496)
XLA Ops:
  19.1 12.1 pad_maximum_fusion
  31.2 12.5 all-gather.47.cloned.1.call-done
  62.0 18.5 all-gather.49.cloned.1.call-done
  89.4 19.9 all-gather.51.cloned.1.call-done
  124.1 27.4 %reduce-scatter.16.cloned.1.call-done = bf16[64,2048]{1,0:T(8,128)(2,1)} async-done(((bf16[256,2048]{1,0:T(8,128)(2,1)}), bf16[64,2048]{1,0:T(8,128)(2,1)}) %reduce-scatter.16.cloned.1.call-update) | async-done | bytes 262160 | tf_op jit(solution)/shard_map/reduce_scatter | solution.py:173
  156.8 27.9 %all-gather.53.cloned.1.call-done = bf16[256,2048]{1,0:T(8,128)(2,1)} async-done(((bf16[64,2048]{1,0:T(8,128)(2,1)}), bf16[256,2048]{1,0:T(8,128)(2,1)}) %all-gather.53.cloned.1.call-update) | async-done | bytes 1048592 | tf_op jit(solution)/shard_map/all_gather | solution.py:130
  215.8 13.5 all-gather.55.cloned.1.call-done
  238.3 19.2 all-gather.57.cloned.1.call-done
  275.1 26.7 %reduce-scatter.18.cloned.1.call-done = bf16[64,2048]{1,0:T(8,128)(2,1)} async-done(((bf16[256,2048]{1,0:T(8,128)(2,1)}), bf16[64,2048]{1,0:T(8,128)(2,1)}) %reduce-scatter.18.cloned.1.call-update) | async-done | bytes 262160 | tf_op jit(solution)/shard_map/reduce_scatter | solution.py:173
  308.2 27.7 %all-gather.59.cloned.1.call-done = bf16[256,2048]{1,0:T(8,128)(2,1)} async-done(((bf16[64,2048]{1,0:T(8,128)(2,1)}), bf16[256,2048]{1,0:T(8,128)(2,1)}) %all-gather.59.cloned.1.call-update) | async-done | bytes 1048592 | tf_op jit(solution)/shard_map/all_gather | solution.py:130
  363.1 17.4 all-gather.61.cloned.1.call-done
  389.5 19.2 all-gather.63.cloned.1.call-done
  426.3 26.7 %reduce-scatter.20.cloned.1.call-done = bf16[64,2048]{1,0:T(8,128)(2,1)} async-done(((bf16[256,2048]{1,0:T(8,128)(2,1)}), bf16[64,2048]{1,0:T(8,128)(2,1)}) %reduce-scatter.20.cloned.1.call-update) | async-done | bytes 262160 | tf_op jit(solution)/shard_map/reduce_scatter | solution.py:173
  459.6 27.5 %all-gather.65.cloned.1.call-done = bf16[256,2048]{1,0:T(8,128)(2,1)} async-done(((bf16[64,2048]{1,0:T(8,128)(2,1)}), bf16[256,2048]{1,0:T(8,128)(2,1)}) %all-gather.65.cloned.1.call-update) | async-done | bytes 1048592 | tf_op jit(solution)/shard_map/all_gather | solution.py:130
  516.7 14.9 all-gather.67.cloned.1.call-done
  540.7 19.0 all-gather.69.cloned.1.call-done
  598.6 19.9 reduce-scatter.22.cloned.1.call-done
  641.5 11.1 all-gather.71.cloned.1.call-done
  732.7 20.9 all-gather.95.cloned.1.call-done
  762.5 19.2 all-gather.99.cloned.1.call-done
  816.8 10.0 reduce-scatter.26.cloned.1.call-done
  842.0 10.6 convolution_convert_fusion.4
  853.4 26.6 %reduce-scatter.28.cloned.1.call-done = bf16[64,2048]{1,0:T(8,128)(2,1)} async-done(((bf16[256,2048]{1,0:T(8,128)(2,1)}), bf16[64,2048]{1,0:T(8,128)(2,1)}) %reduce-scatter.28.cloned.1.call-update) | async-done | bytes 262160 | tf_op jit(solution)/shard_map/reduce_scatter | solution.py:301
  892.1 14.6 all-gather.101.cloned.1.call-done
  912.8 23.4 %all-gather.77.cloned.1.call-done = bf16[256,2048]{1,0:T(8,128)(2,1)} async-done(((bf16[64,2048]{1,0:T(8,128)(2,1)}), bf16[256,2048]{1,0:T(8,128)(2,1)}) %all-gather.77.cloned.1.call-update) | async-done | bytes 1048592 | tf_op jit(solution)/shard_map/all_gather | solution.py:219
  952.3 11.3 all-gather.103.cloned.1.call-done
  983.3 25.3 %reduce-scatter.30.cloned.1.call-done = bf16[256,1024]{0,1:T(8,128)(2,1)} async-done(((bf16[1024,1024]{0,1:T(8,128)(2,1)}), bf16[256,1024]{0,1:T(8,128)(2,1)}) %reduce-scatter.30.cloned.1.call-update) | async-done | bytes 524304 | tf_op jit(solution)/shard_map/reduce_scatter | solution.py:270
  1023.9 10.6 convolution_convert_fusion.3
  1036.9 25.0 %reduce-scatter.32.cloned.1.call-done = bf16[64,2048]{1,0:T(8,128)(2,1)} async-done(((bf16[256,2048]{1,0:T(8,128)(2,1)}), bf16[64,2048]{1,0:T(8,128)(2,1)}) %reduce-scatter.32.cloned.1.call-update) | async-done | bytes 262160 | tf_op jit(solution)/shard_map/reduce_scatter | solution.py:301
  1074.3 14.3 all-gather.105.cloned.1.call-done
  1094.5 23.6 %all-gather.79.cloned.1.call-done = bf16[256,2048]{1,0:T(8,128)(2,1)} async-done(((bf16[64,2048]{1,0:T(8,128)(2,1)}), bf16[256,2048]{1,0:T(8,128)(2,1)}) %all-gather.79.cloned.1.call-update) | async-done | bytes 1048592 | tf_op jit(solution)/shard_map/all_gather | solution.py:219
  1135.9 9.9 all-gather.107.cloned.1.call-done
  1165.6 25.3 %reduce-scatter.34.cloned.1.call-done = bf16[256,1024]{0,1:T(8,128)(2,1)} async-done(((bf16[1024,1024]{0,1:T(8,128)(2,1)}), bf16[256,1024]{0,1:T(8,128)(2,1)}) %reduce-scatter.34.cloned.1.call-update) | async-done | bytes 524304 | tf_op jit(solution)/shard_map/reduce_scatter | solution.py:270
  1206.6 10.7 convolution_convert_fusion.2
  1219.8 25.0 %reduce-scatter.36.cloned.1.call-done = bf16[64,2048]{1,0:T(8,128)(2,1)} async-done(((bf16[256,2048]{1,0:T(8,128)(2,1)}), bf16[64,2048]{1,0:T(8,128)(2,1)}) %reduce-scatter.36.cloned.1.call-update) | async-done | bytes 262160 | tf_op jit(solution)/shard_map/reduce_scatter | solution.py:301
  1255.8 15.8 all-gather.109.cloned.1.call-done
  1277.5 23.4 %all-gather.81.cloned.1.call-done = bf16[256,2048]{1,0:T(8,128)(2,1)} async-done(((bf16[64,2048]{1,0:T(8,128)(2,1)}), bf16[256,2048]{1,0:T(8,128)(2,1)}) %all-gather.81.cloned.1.call-update) | async-done | bytes 1048592 | tf_op jit(solution)/shard_map/all_gather | solution.py:219
  1318.7 9.7 all-gather.111.cloned.1.call-done
  1348.1 25.4 %reduce-scatter.38.cloned.1.call-done = bf16[256,1024]{0,1:T(8,128)(2,1)} async-done(((bf16[1024,1024]{0,1:T(8,128)(2,1)}), bf16[256,1024]{0,1:T(8,128)(2,1)}) %reduce-scatter.38.cloned.1.call-update) | async-done | bytes 524304 | tf_op jit(solution)/shard_map/reduce_scatter | solution.py:270
  1389.3 10.7 convolution_convert_fusion.1
  1402.5 25.0 %reduce-scatter.40.cloned.1.call-done = bf16[64,2048]{1,0:T(8,128)(2,1)} async-done(((bf16[256,2048]{1,0:T(8,128)(2,1)}), bf16[64,2048]{1,0:T(8,128)(2,1)}) %reduce-scatter.40.cloned.1.call-update) | async-done | bytes 262160 | tf_op jit(solution)/shard_map/reduce_scatter | solution.py:301
  1440.0 14.2 all-gather.113.cloned.1.call-done
  1460.5 23.3 %all-gather.83.cloned.1.call-done = bf16[256,2048]{1,0:T(8,128)(2,1)} async-done(((bf16[64,2048]{1,0:T(8,128)(2,1)}), bf16[256,2048]{1,0:T(8,128)(2,1)}) %all-gather.83.cloned.1.call-update) | async-done | bytes 1048592 | tf_op jit(solution)/shard_map/all_gather | solution.py:219
  1492.0 19.4 all-gather.115.cloned.1.call-done
  1560.2 10.0 fusion.197
  1570.1 10.3 fusion.195
  1580.5 15.2 fusion.526
  1595.8 13.7 fusion.527
  1609.5 10.1 fusion.193
  1619.7 13.6 fusion.525
  1633.3 10.3 fusion.191
  1643.6 15.6 fusion.524
  1661.5 26.5 %add_convert_fusion.1 = bf16[2560,2048]{1,0:T(8,128)(2,1)} fusion(f32[2560,2048]{1,0:T(8,128)} %fusion.191, f32[2560,2048]{1,0:T(8,128)} %fusion.193, f32[2560,2048]{1,0:T(8,128)} %fusion.195, f32[2560,2048]{1,0:T(8,128)} %fusion.197, bf16[256,2048]{1,0:T(8,128)(2,1)} %all-gather.83.cloned.1.call-done, pred[]{:T(512)S(6)} %and.120, pred[]{:T(512)S(6)} %and.118, ...), kind=kOutput, calls=%fused_computation.1 | convolution fusion | flops 2736783360 | bytes 96731144 | tf_op jit(solution)/shard_map/dot_general | solution.py:220
  1701.1 10.3 convolution_convert_fusion
  1711.5 35.0 %add_convert_fusion = bf16[2048,3584]{1,0:T(8,128)(2,1)} fusion(f32[2048,3584]{1,0:T(8,128)} %fusion.524, f32[2048,3584]{1,0:T(8,128)} %fusion.525, f32[2048,3584]{1,0:T(8,128)} %fusion.526, f32[2048,3584]{1,0:T(8,128)} %fusion.527, bf16[256,2048]{1,0:T(8,128)(2,1)} %all-gather.93.cloned.1.call-done, pred[]{:T(512)S(6)} %and.120, pred[]{:T(512)S(6)} %and.118, ...), kind=kOutput, calls=%fused_computation | convolution fusion | flops 3838836736 | bytes 135004160 | tf_op jit(solution)/shard_map/dot_general | solution.py:295
  1758.1 16.3 all-reduce.1
  1775.6 19.8 all-reduce
  1796.9 407.8 %all-reduce.5.cloned.1.call-done = (bf16[2048,3584]{1,0:T(8,128)(2,1)}, bf16[2560,2048]{1,0:T(8,128)(2,1)}) async-done(((bf16[2048,3584]{1,0:T(8,128)(2,1)}, bf16[2560,2048]{1,0:T(8,128)(2,1)}), (bf16[2048,3584]{1,0:T(8,128)(2,1)}, bf16[2560,2048]{1,0:T(8,128)(2,1)})) %all-reduce.5.cloned.1.call-update) | async-done | bytes 25165840 | tf_op jit(solution)/shard_map/psum | solution.py:328
  2204.7 10.4 slice.551
  2215.1 10.9 convert_element_type.722
  2226.0 13.8 convert_element_type.735
  2244.5 12.6 copy.144
  2257.1 12.6 copy.150
  2269.7 21.2 slice_bitcast_fusion
  (873 shorter events, 749.9 us)
Async XLA Ops:
  7.2 36.5 %all-gather.47.cloned.1.call-start = ((), (), s32[]{:S(2)}) async-start(), calls=%async_computation.15 | async-start | bytes 1310720 | tf_op jit(solution)/shard_map/all_gather | solution.py:130
  10.3 1419.0 %copy-start.82 = (f32[1,2048]{1,0:T(1,128)}, f32[1,2048]{1,0:T(1,128)S(1)}, u32[]{:S(2)}) copy-start(f32[1,2048]{1,0:T(1,128)S(1)} %mul.1491) | copy-start | bytes 24580
  12.8 67.7 %all-gather.49.cloned.1.call-start = ((), (), s32[]{:S(2)}) async-start(), calls=%async_computation.16 | async-start | bytes 1310720 | tf_op jit(solution)/shard_map/all_gather | solution.py:146
  19.1 1361.6 %copy-start.88 = (f32[256,16]{0,1:T(8,128)}, f32[256,16]{0,1:T(8,128)S(1)}, u32[]{:S(2)}) copy-start(f32[256,16]{0,1:T(8,128)S(1)} %get-tuple-element.213) | copy-start | bytes 49156
  19.1 1361.5 %copy-start.90 = (f32[256,16]{0,1:T(8,128)}, f32[256,16]{0,1:T(8,128)S(1)}, u32[]{:S(2)}) copy-start(f32[256,16]{0,1:T(8,128)S(1)} %get-tuple-element.214) | copy-start | bytes 49156
  54.6 54.7 %all-gather.51.cloned.1.call-start = ((), (), s32[]{:S(2)}) async-start(), calls=%async_computation.17 | async-start | bytes 1310720 | tf_op jit(solution)/shard_map/all_gather | solution.py:147
  59.1 92.4 %reduce-scatter.16.cloned.1.call-start = ((), (), s32[]{:S(2)}) async-start(), calls=%async_computation.18 | async-start | bytes 1310720 | tf_op jit(solution)/shard_map/reduce_scatter | solution.py:173
  124.0 60.7 %all-gather.53.cloned.1.call-start = ((), (), s32[]{:S(2)}) async-start(), calls=%async_computation.19 | async-start | bytes 1310720 | tf_op jit(solution)/shard_map/all_gather | solution.py:130
  152.7 2.6 collective-permute-start
  156.7 72.6 %all-gather.55.cloned.1.call-start = ((), (), s32[]{:S(2)}) async-start(), calls=%async_computation.20 | async-start | bytes 1310720 | tf_op jit(solution)/shard_map/all_gather | solution.py:146
  203.4 54.1 %all-gather.57.cloned.1.call-start = ((), (), s32[]{:S(2)}) async-start(), calls=%async_computation.21 | async-start | bytes 1310720 | tf_op jit(solution)/shard_map/all_gather | solution.py:147
  210.9 90.9 %reduce-scatter.18.cloned.1.call-start = ((), (), s32[]{:S(2)}) async-start(), calls=%async_computation.22 | async-start | bytes 1310720 | tf_op jit(solution)/shard_map/reduce_scatter | solution.py:173
  274.4 61.5 %all-gather.59.cloned.1.call-start = ((), (), s32[]{:S(2)}) async-start(), calls=%async_computation.23 | async-start | bytes 1310720 | tf_op jit(solution)/shard_map/all_gather | solution.py:130
  303.7 2.8 collective-permute-start.1
  307.9 72.6 %all-gather.61.cloned.1.call-start = ((), (), s32[]{:S(2)}) async-start(), calls=%async_computation.24 | async-start | bytes 1310720 | tf_op jit(solution)/shard_map/all_gather | solution.py:146
  354.6 54.2 %all-gather.63.cloned.1.call-start = ((), (), s32[]{:S(2)}) async-start(), calls=%async_computation.25 | async-start | bytes 1310720 | tf_op jit(solution)/shard_map/all_gather | solution.py:147
  358.2 94.8 %reduce-scatter.20.cloned.1.call-start = ((), (), s32[]{:S(2)}) async-start(), calls=%async_computation.26 | async-start | bytes 1310720 | tf_op jit(solution)/shard_map/reduce_scatter | solution.py:173
  425.6 61.5 %all-gather.65.cloned.1.call-start = ((), (), s32[]{:S(2)}) async-start(), calls=%async_computation.27 | async-start | bytes 1310720 | tf_op jit(solution)/shard_map/all_gather | solution.py:130
  454.9 2.8 collective-permute-start.2
  459.1 72.5 %all-gather.67.cloned.1.call-start = ((), (), s32[]{:S(2)}) async-start(), calls=%async_computation.28 | async-start | bytes 1310720 | tf_op jit(solution)/shard_map/all_gather | solution.py:146
  505.7 54.0 %all-gather.69.cloned.1.call-start = ((), (), s32[]{:S(2)}) async-start(), calls=%async_computation.29 | async-start | bytes 1310720 | tf_op jit(solution)/shard_map/all_gather | solution.py:147
  509.4 79.8 %all-gather.97.cloned.1.call-start = ((), (), s32[]{:S(2)}) async-start(), calls=%async_computation.55 | async-start | bytes 1310720 | tf_op jit(solution)/shard_map/all_gather | solution.py:219
  511.7 106.8 %reduce-scatter.22.cloned.1.call-start = ((), (), s32[]{:S(2)}) async-start(), calls=%async_computation.30 | async-start | bytes 1310720 | tf_op jit(solution)/shard_map/reduce_scatter | solution.py:173
  576.7 75.9 %all-gather.71.cloned.1.call-start = ((), (), s32[]{:S(2)}) async-start(), calls=%async_computation.31 | async-start | bytes 1310720 | tf_op jit(solution)/shard_map/all_gather | solution.py:130
  619.7 4.2 collective-permute-start.3
  624.0 805.3 %copy-start.1 = (bf16[4,64,2048]{2,1,0:T(8,128)(2,1)}, bf16[4,64,2048]{2,1,0:T(8,128)(2,1)S(1)}, u32[]{:S(2)}) copy-start(bf16[4,64,2048]{2,1,0:T(8,128)(2,1)S(1)} %get-tuple-element.78) | copy-start | bytes 3145732
  625.6 85.4 %all-gather.73.cloned.1.call-start = ((), (), s32[]{:S(2)}) async-start(), calls=%async_computation.32 | async-start | bytes 1310720 | tf_op jit(solution)/shard_map/all_gather | solution.py:146
  671.3 54.0 %all-gather.75.cloned.1.call-start = ((), (), s32[]{:S(2)}) async-start(), calls=%async_computation.33 | async-start | bytes 1310720 | tf_op jit(solution)/shard_map/all_gather | solution.py:147
  685.2 68.3 %all-gather.95.cloned.1.call-start = ((), (), s32[]{:S(2)}) async-start(), calls=%async_computation.54 | async-start | bytes 1310720 | tf_op jit(solution)/shard_map/all_gather | solution.py:233
  697.6 84.1 %all-gather.99.cloned.1.call-start = ((), (), s32[]{:S(2)}) async-start(), calls=%async_computation.56 | async-start | bytes 1310720 | tf_op jit(solution)/shard_map/all_gather | solution.py:234
  709.0 117.8 %reduce-scatter.26.cloned.1.call-start = ((), (), s32[]{:S(2)}) async-start(), calls=%async_computation.35 | async-start | bytes 2621440 | tf_op jit(solution)/shard_map/reduce_scatter | solution.py:270
  791.4 88.6 %reduce-scatter.28.cloned.1.call-start = ((), (), s32[]{:S(2)}) async-start(), calls=%async_computation.36 | async-start | bytes 1310720 | tf_op jit(solution)/shard_map/reduce_scatter | solution.py:301
  852.6 54.2 %all-gather.101.cloned.1.call-start = ((), (), s32[]{:S(2)}) async-start(), calls=%async_computation.57 | async-start | bytes 1310720 | tf_op jit(solution)/shard_map/all_gather | solution.py:233
  853.3 82.9 %all-gather.77.cloned.1.call-start = ((), (), s32[]{:S(2)}) async-start(), calls=%async_computation.37 | async-start | bytes 1310720 | tf_op jit(solution)/shard_map/all_gather | solution.py:219
  885.6 3.4 collective-permute-start.4
  891.3 72.3 %all-gather.103.cloned.1.call-start = ((), (), s32[]{:S(2)}) async-start(), calls=%async_computation.58 | async-start | bytes 1310720 | tf_op jit(solution)/shard_map/all_gather | solution.py:234
  891.9 116.8 %reduce-scatter.30.cloned.1.call-start = ((), (), s32[]{:S(2)}) async-start(), calls=%async_computation.38 | async-start | bytes 2621440 | tf_op jit(solution)/shard_map/reduce_scatter | solution.py:270
  973.3 88.6 %reduce-scatter.32.cloned.1.call-start = ((), (), s32[]{:S(2)}) async-start(), calls=%async_computation.39 | async-start | bytes 1310720 | tf_op jit(solution)/shard_map/reduce_scatter | solution.py:301
  1015.1 565.4 %copy-start.46 = (bf16[256,512]{1,0:T(8,128)(2,1)}, bf16[256,512]{1,0:T(8,128)(2,1)S(1)}, u32[]{:S(2)}) copy-start(bf16[256,512]{1,0:T(8,128)(2,1)S(1)} %copy.131) | copy-start | bytes 786436
  1034.5 54.0 %all-gather.105.cloned.1.call-start = ((), (), s32[]{:S(2)}) async-start(), calls=%async_computation.59 | async-start | bytes 1310720 | tf_op jit(solution)/shard_map/all_gather | solution.py:233
  1035.1 83.0 %all-gather.79.cloned.1.call-start = ((), (), s32[]{:S(2)}) async-start(), calls=%async_computation.40 | async-start | bytes 1310720 | tf_op jit(solution)/shard_map/all_gather | solution.py:219
  1067.5 3.4 collective-permute-start.5
  1073.2 72.5 %all-gather.107.cloned.1.call-start = ((), (), s32[]{:S(2)}) async-start(), calls=%async_computation.60 | async-start | bytes 1310720 | tf_op jit(solution)/shard_map/all_gather | solution.py:234
  1074.0 116.9 %reduce-scatter.34.cloned.1.call-start = ((), (), s32[]{:S(2)}) async-start(), calls=%async_computation.41 | async-start | bytes 2621440 | tf_op jit(solution)/shard_map/reduce_scatter | solution.py:270
  1155.5 89.3 %reduce-scatter.36.cloned.1.call-start = ((), (), s32[]{:S(2)}) async-start(), calls=%async_computation.42 | async-start | bytes 1310720 | tf_op jit(solution)/shard_map/reduce_scatter | solution.py:301
  1217.3 54.2 %all-gather.109.cloned.1.call-start = ((), (), s32[]{:S(2)}) async-start(), calls=%async_computation.61 | async-start | bytes 1310720 | tf_op jit(solution)/shard_map/all_gather | solution.py:233
  1218.1 82.9 %all-gather.81.cloned.1.call-start = ((), (), s32[]{:S(2)}) async-start(), calls=%async_computation.43 | async-start | bytes 1310720 | tf_op jit(solution)/shard_map/all_gather | solution.py:219
  1248.9 3.4 collective-permute-start.6
  1254.6 73.8 %all-gather.111.cloned.1.call-start = ((), (), s32[]{:S(2)}) async-start(), calls=%async_computation.62 | async-start | bytes 1310720 | tf_op jit(solution)/shard_map/all_gather | solution.py:234
  1255.2 118.3 %reduce-scatter.38.cloned.1.call-start = ((), (), s32[]{:S(2)}) async-start(), calls=%async_computation.44 | async-start | bytes 2621440 | tf_op jit(solution)/shard_map/reduce_scatter | solution.py:270
  1338.2 89.3 %reduce-scatter.40.cloned.1.call-start = ((), (), s32[]{:S(2)}) async-start(), calls=%async_computation.45 | async-start | bytes 1310720 | tf_op jit(solution)/shard_map/reduce_scatter | solution.py:301
  1400.0 54.2 %all-gather.113.cloned.1.call-start = ((), (), s32[]{:S(2)}) async-start(), calls=%async_computation.63 | async-start | bytes 1310720 | tf_op jit(solution)/shard_map/all_gather | solution.py:233
  1400.7 83.0 %all-gather.83.cloned.1.call-start = ((), (), s32[]{:S(2)}) async-start(), calls=%async_computation.46 | async-start | bytes 1310720 | tf_op jit(solution)/shard_map/all_gather | solution.py:219
  1431.5 3.4 collective-permute-start.7
  1437.3 74.1 %all-gather.115.cloned.1.call-start = ((), (), s32[]{:S(2)}) async-start(), calls=%async_computation.64 | async-start | bytes 1310720 | tf_op jit(solution)/shard_map/all_gather | solution.py:234
  1438.0 142.5 %all-gather.87.cloned.1.call-start = ((), (), s32[]{:S(2)}) async-start(), calls=%async_computation.50 | async-start | bytes 1310720 | tf_op jit(solution)/shard_map/all_gather | solution.py:296
  1438.6 157.2 %all-gather.85.cloned.1.call-start = ((), (), s32[]{:S(2)}) async-start(), calls=%async_computation.49 | async-start | bytes 1310720 | tf_op jit(solution)/shard_map/all_gather | solution.py:296
  1439.3 180.3 %all-gather.89.cloned.1.call-start = ((), (), s32[]{:S(2)}) async-start(), calls=%async_computation.51 | async-start | bytes 1310720 | tf_op jit(solution)/shard_map/all_gather | solution.py:296
  1439.9 203.6 %all-gather.91.cloned.1.call-start = ((), (), s32[]{:S(2)}) async-start(), calls=%async_computation.52 | async-start | bytes 1310720 | tf_op jit(solution)/shard_map/all_gather | solution.py:296
  1460.2 231.3 %reduce-scatter.42.cloned.1.call-start = ((), (), s32[]{:S(2)}) async-start(), calls=%async_computation.47 | async-start | bytes 2621440 | tf_op jit(solution)/shard_map/reduce_scatter | solution.py:270
  1526.3 185.2 %all-gather.93.cloned.1.call-start = ((), (), s32[]{:S(2)}) async-start(), calls=%async_computation.53 | async-start | bytes 1310720 | tf_op jit(solution)/shard_map/all_gather | solution.py:296
  1544.1 204.9 %reduce-scatter.24.cloned.1.call-start = ((), (), s32[]{:S(2)}) async-start(), calls=%async_computation.34 | async-start | bytes 1310720 | tf_op jit(solution)/shard_map/reduce_scatter | solution.py:173
  1557.3 199.2 %reduce-scatter.44.cloned.1.call-start = ((), (), s32[]{:S(2)}) async-start(), calls=%async_computation.48 | async-start | bytes 1310720 | tf_op jit(solution)/shard_map/reduce_scatter | solution.py:301
  1711.4 493.2 %all-reduce.5.cloned.1.call-start = ((), (), s32[]{:S(2)}) async-start(), calls=%async_computation.65 | async-start | bytes 50331648 | tf_op jit(solution)/shard_map/psum | solution.py:328
  (177 other events, 2886.0 us)
Sparse Core Ops, SparseCore 0:
  13.0 30.6 all-gather.46
  54.7 25.7 all-gather.48
  82.9 26.3 all-gather.50
  124.1 27.2 reduce-scatter.15
  156.8 27.7 all-gather.52
  203.5 25.7 all-gather.54
  231.1 26.3 all-gather.56
  274.5 27.2 reduce-scatter.17
  308.0 27.7 all-gather.58
  354.7 25.7 all-gather.60
  382.3 26.3 all-gather.62
  425.7 27.2 reduce-scatter.19
  459.2 27.7 all-gather.64
  505.8 25.7 all-gather.66
  533.3 26.3 all-gather.68
  561.1 27.9 all-gather.96
  591.8 26.6 reduce-scatter.21
  625.7 26.8 all-gather.70
  671.4 25.7 all-gather.72
  698.9 26.3 all-gather.74
  727.1 26.3 all-gather.94
  755.3 26.3 all-gather.98
  791.5 35.1 reduce-scatter.25
  852.7 27.2 reduce-scatter.27
  881.9 24.8 all-gather.100
  908.2 27.9 all-gather.76
  937.9 25.7 all-gather.102
  973.4 35.1 reduce-scatter.29
  1034.6 27.2 reduce-scatter.31
  1063.6 24.8 all-gather.104
  1090.1 27.9 all-gather.78
  1120.0 25.7 all-gather.106
  1155.6 35.1 reduce-scatter.33
  1217.5 27.2 reduce-scatter.35
  1246.6 24.8 all-gather.108
  1272.9 27.9 all-gather.80
  1302.6 25.7 all-gather.110
  1338.3 35.1 reduce-scatter.37
  1400.1 27.2 reduce-scatter.39
  1429.3 24.8 all-gather.112
  1455.8 27.9 all-gather.82
  1485.6 25.7 all-gather.114
  1512.8 27.9 all-gather.86
  1542.4 27.3 all-gather.84
  1571.2 27.3 all-gather.88
  1600.0 27.3 all-gather.90
  1630.2 34.5 reduce-scatter.41
  1666.2 27.9 all-gather.92
  1696.4 26.6 reduce-scatter.23
  1726.0 25.7 reduce-scatter.43
  1756.0 448.6 all-reduce.4
where the time goes:
time: 2310 us; the launch traced here: 2300 us
  waiting for transfers between devices  1210 us (52%)
  matrix products  482 us (21%)
  local copies, waits for them, and re-layouts  269 us (12%)
  other arithmetic  261 us (11%)
  blocking collectives  36.1 us (2%)
    psum x1, waiting for transfers between devices, on_device(): lax.psum(total_w_in.astype(jnp.bfloat16), 'ctx').astype(jnp.float32)  408 us
    all_gather x5, waiting for transfers between devices, on_device(): lax.all_gather(normed_b, 'tp', axis=0, tiled=True)  107 us
    reduce_scatter x5, waiting for transfers between devices, on_device(): lax.psum_scatter(lax.dot_general(grad_proj_b, w_in, contract_cols, prefer...  102 us
    reduce_scatter x5, waiting for transfers between devices, on_device(): lax.psum_scatter(jnp.dot(branch_in, w_out, preferred_element_type=jnp.flo...  101 us
    all_gather x5, waiting for transfers between devices, on_device(): fold_pieces = lax.all_gather(grad_out_b, 'tp', axis=0, tiled=True)  93.7 us
    dot_general x5, matrix products, on_device(): lax.dot_general(lax.all_gather(backward_normed_b, 'tp', axis=0, tiled=Tru...  93.2 us
    reduce_scatter x5, waiting for transfers between devices, on_device(): lax.psum_scatter(jnp.concatenate([grad_key_part, grad_value_part], axis=2...  86 us
    all_gather x5, waiting for transfers between devices, on_device(): values_part = lax.all_gather(values_b, 'ctx', axis=0, tiled=True)  85.2 us
  transfers between devices with their start and end apart: 59, of which 48 were waited for; matrix products, arithmetic and copies ran while one was open for 26% of the time, Pallas kernels for 0%

commit v1 on v0

--- a/solution.py
+++ b/solution.py
@@ -325,7 +325,7 @@
         received = from_behind(grad_x_b, "section", -1)
     total_w_in, total_w_out, total_bias_in, total_gain, total_shift, total_bias_out = totals
     sum_w_in, sum_w_out, sum_bias_in, sum_gain, sum_shift, sum_bias_out = (
-        lax.psum(total_w_in.astype(jnp.bfloat16), "ctx").astype(jnp.float32),
+        jnp.sum(lax.all_gather(total_w_in.astype(jnp.bfloat16), "ctx"), axis=0).astype(jnp.float32),
         lax.psum(total_w_out.astype(jnp.bfloat16), "ctx").astype(jnp.float32),
         lax.psum(total_bias_in.astype(jnp.bfloat16), "ctx").astype(jnp.float32),
         lax.psum(total_gain.astype(jnp.bfloat16), "ctx").astype(jnp.float32),

time: 2310 us -> 2580 us (1.12)
  waiting for transfers between devices: 1210 us -> 1450 us
  other arithmetic: 261 us -> 294 us
    all_gather x0 -> x1, waiting for transfers between devices: none -> 468 us  [on_device(): lax.all_gather(total_w_in.astype(jnp.bfloat16), 'ctx')]
    psum x1, waiting for transfers between devices: 408 us -> 171 us  [on_device(): lax.psum(total_w_out.astype(jnp.bfloat16), 'ctx').astype(jnp.float32)]
    reduce_sum x0 -> x1, other arithmetic: none -> 27.6 us  [on_device(): jnp.sum(lax.all_gather(total_w_in.astype(jnp.bfloat16), 'ctx'), axis=0)]
    unnamed x367 -> x349, local copies, waits for them, and re-layouts: 64.8 us -> 65.4 us
  transfers between devices with their start and end apart: 59 -> 60, of which waited for: 48 -> 50; matrix products, arithmetic and copies ran while one was open for 26% -> 24% of each run, Pallas kernels for 0% -> 0%
where the time goes in v1:
time: 2580 us; the launch traced here: 2570 us
  waiting for transfers between devices  1450 us (56%)
  matrix products  485 us (19%)
  other arithmetic  294 us (11%)
  local copies, waits for them, and re-layouts  269 us (10%)
  blocking collectives  34.3 us (1%)
    all_gather x1, waiting for transfers between devices, on_device(): lax.all_gather(total_w_in.astype(jnp.bfloat16), 'ctx')  468 us
    psum x1, waiting for transfers between devices, on_device(): lax.psum(total_w_out.astype(jnp.bfloat16), 'ctx').astype(jnp.float32)  171 us
    reduce_scatter x5, waiting for transfers between devices, on_device(): lax.psum_scatter(lax.dot_general(grad_proj_b, w_in, contract_cols, prefer...  108 us
    all_gather x5, waiting for transfers between devices, on_device(): lax.all_gather(normed_b, 'tp', axis=0, tiled=True)  107 us
    reduce_scatter x5, waiting for transfers between devices, on_device(): lax.psum_scatter(jnp.dot(branch_in, w_out, preferred_element_type=jnp.flo...  101 us
    dot_general x5, matrix products, on_device(): lax.dot_general(lax.all_gather(backward_normed_b, 'tp', axis=0, tiled=Tru...  96.8 us
    all_gather x5, waiting for transfers between devices, on_device(): fold_pieces = lax.all_gather(grad_out_b, 'tp', axis=0, tiled=True)  94.1 us
    reduce_scatter x5, waiting for transfers between devices, on_device(): lax.psum_scatter(jnp.concatenate([grad_key_part, grad_value_part], axis=2...  86.2 us
  transfers between devices with their start and end apart: 60, of which 50 were waited for; matrix products, arithmetic and copies ran while one was open for 24% of the time, Pallas kernels for 0%

profile of v1, /device:TPU:0, one launch (start us, length us, event | category | flops | bytes accessed | tf_op | source)
XLA Modules:
  0.0 2569.4 jit_solution(2942703494254616139)
XLA Ops:
  19.1 12.1 pad_maximum_fusion
  31.2 12.5 all-gather.49.cloned.1.call-done
  61.6 18.9 all-gather.51.cloned.1.call-done
  89.4 19.9 all-gather.53.cloned.1.call-done
  124.1 27.4 %reduce-scatter.16.cloned.1.call-done = bf16[64,2048]{1,0:T(8,128)(2,1)} async-done(((bf16[256,2048]{1,0:T(8,128)(2,1)}), bf16[64,2048]{1,0:T(8,128)(2,1)}) %reduce-scatter.16.cloned.1.call-update) | async-done | bytes 262160 | tf_op jit(solution)/shard_map/reduce_scatter | solution.py:173
  156.8 27.9 %all-gather.55.cloned.1.call-done = bf16[256,2048]{1,0:T(8,128)(2,1)} async-done(((bf16[64,2048]{1,0:T(8,128)(2,1)}), bf16[256,2048]{1,0:T(8,128)(2,1)}) %all-gather.55.cloned.1.call-update) | async-done | bytes 1048592 | tf_op jit(solution)/shard_map/all_gather | solution.py:130
  215.8 13.5 all-gather.57.cloned.1.call-done
  238.3 19.2 all-gather.59.cloned.1.call-done
  275.1 26.7 %reduce-scatter.18.cloned.1.call-done = bf16[64,2048]{1,0:T(8,128)(2,1)} async-done(((bf16[256,2048]{1,0:T(8,128)(2,1)}), bf16[64,2048]{1,0:T(8,128)(2,1)}) %reduce-scatter.18.cloned.1.call-update) | async-done | bytes 262160 | tf_op jit(solution)/shard_map/reduce_scatter | solution.py:173
  308.3 27.5 %all-gather.61.cloned.1.call-done = bf16[256,2048]{1,0:T(8,128)(2,1)} async-done(((bf16[64,2048]{1,0:T(8,128)(2,1)}), bf16[256,2048]{1,0:T(8,128)(2,1)}) %all-gather.61.cloned.1.call-update) | async-done | bytes 1048592 | tf_op jit(solution)/shard_map/all_gather | solution.py:130
  363.2 17.4 all-gather.63.cloned.1.call-done
  389.6 19.2 all-gather.65.cloned.1.call-done
  426.4 26.7 %reduce-scatter.20.cloned.1.call-done = bf16[64,2048]{1,0:T(8,128)(2,1)} async-done(((bf16[256,2048]{1,0:T(8,128)(2,1)}), bf16[64,2048]{1,0:T(8,128)(2,1)}) %reduce-scatter.20.cloned.1.call-update) | async-done | bytes 262160 | tf_op jit(solution)/shard_map/reduce_scatter | solution.py:173
  459.4 27.7 %all-gather.67.cloned.1.call-done = bf16[256,2048]{1,0:T(8,128)(2,1)} async-done(((bf16[64,2048]{1,0:T(8,128)(2,1)}), bf16[256,2048]{1,0:T(8,128)(2,1)}) %all-gather.67.cloned.1.call-update) | async-done | bytes 1048592 | tf_op jit(solution)/shard_map/all_gather | solution.py:130
  516.7 14.9 all-gather.69.cloned.1.call-done
  540.7 19.0 all-gather.71.cloned.1.call-done
  598.6 20.0 reduce-scatter.22.cloned.1.call-done
  641.6 11.0 all-gather.73.cloned.1.call-done
  732.7 20.9 all-gather.97.cloned.1.call-done
  762.6 19.2 all-gather.101.cloned.1.call-done
  816.6 10.3 reduce-scatter.26.cloned.1.call-done
  842.0 10.6 convolution_convert_fusion.4
  853.4 26.6 %reduce-scatter.28.cloned.1.call-done = bf16[64,2048]{1,0:T(8,128)(2,1)} async-done(((bf16[256,2048]{1,0:T(8,128)(2,1)}), bf16[64,2048]{1,0:T(8,128)(2,1)}) %reduce-scatter.28.cloned.1.call-update) | async-done | bytes 262160 | tf_op jit(solution)/shard_map/reduce_scatter | solution.py:301
  892.2 14.6 all-gather.103.cloned.1.call-done
  912.8 23.4 all-gather.79.cloned.1.call-done
  952.3 11.4 all-gather.105.cloned.1.call-done
  983.4 25.3 reduce-scatter.30.cloned.1.call-done
  1023.9 10.6 convolution_convert_fusion.3
  1037.0 25.0 reduce-scatter.32.cloned.1.call-done
  1074.5 14.1 all-gather.107.cloned.1.call-done
  1094.6 23.6 all-gather.81.cloned.1.call-done
  1134.4 11.4 all-gather.109.cloned.1.call-done
  1165.5 25.3 reduce-scatter.34.cloned.1.call-done
  1206.0 10.6 convolution_convert_fusion.2
  1218.4 25.7 reduce-scatter.36.cloned.1.call-done
  1254.7 16.1 all-gather.111.cloned.1.call-done
  1276.9 23.4 all-gather.83.cloned.1.call-done
  1316.4 11.4 all-gather.113.cloned.1.call-done
  1347.4 25.3 reduce-scatter.38.cloned.1.call-done
  1388.0 10.6 convolution_convert_fusion.1
  1400.4 25.7 reduce-scatter.40.cloned.1.call-done
  1437.1 15.7 all-gather.115.cloned.1.call-done
  1458.8 23.6 all-gather.85.cloned.1.call-done
  1496.0 14.0 all-gather.117.cloned.1.call-done
  1587.1 10.3 fusion.191
  1607.3 10.2 convolution_convert_fusion
  1617.6 26.1 %add_convert_fusion.1 = bf16[2560,2048]{1,0:T(8,128)(2,1)} fusion(f32[2560,2048]{1,0:T(8,128)} %fusion.191, f32[2560,2048]{1,0:T(8,128)} %fusion.193, f32[2560,2048]{1,0:T(8,128)} %fusion.195, f32[2560,2048]{1,0:T(8,128)} %fusion.197, bf16[256,2048]{1,0:T(8,128)(2,1)S(1)} %copy-done.86, pred[]{:T(512)S(6)} %and.120, pred[]{:T(512)S(6)} %and.118, ...), kind=kOutput, calls=%fused_computation.1 | convolution fusion | flops 2736783360 | bytes 96731144 | tf_op jit(solution)/shard_map/dot_general | solution.py:220
  1645.0 15.2 fusion.526
  1660.2 15.1 fusion.527
  1675.3 15.6 fusion.525
  1690.9 15.7 fusion.524
  1706.7 35.2 %add_convert_fusion = bf16[2048,3584]{1,0:T(8,128)(2,1)} fusion(f32[2048,3584]{1,0:T(8,128)} %fusion.524, f32[2048,3584]{1,0:T(8,128)} %fusion.525, f32[2048,3584]{1,0:T(8,128)} %fusion.526, f32[2048,3584]{1,0:T(8,128)} %fusion.527, bf16[256,2048]{1,0:T(8,128)(2,1)} %all-gather.95.cloned.1.call-done, pred[]{:T(512)S(6)} %and.120, pred[]{:T(512)S(6)} %and.118, ...), kind=kOutput, calls=%fused_computation | convolution fusion | flops 3838836736 | bytes 135004160 | tf_op jit(solution)/shard_map/dot_general | solution.py:295
  1758.6 17.0 all-reduce.1
  1776.8 17.3 all-reduce
  1795.5 171.1 %all-reduce.4.cloned.1.call-done = bf16[2560,2048]{1,0:T(8,128)(2,1)} async-done(((bf16[2560,2048]{1,0:T(8,128)(2,1)}), bf16[2560,2048]{1,0:T(8,128)(2,1)}) %all-reduce.4.cloned.1.call-update) | async-done | bytes 10485776 | tf_op jit(solution)/shard_map/psum | solution.py:329
  1966.6 20.2 convert_element_type.737
  1993.2 15.3 slice_bitcast_fusion
  2008.4 468.1 %all-gather.119.cloned.1.call-done = bf16[8192,3584]{1,0:T(8,128)(2,1)} async-done(((bf16[2048,3584]{1,0:T(8,128)(2,1)}), bf16[8192,3584]{1,0:T(8,128)(2,1)}) %all-gather.119.cloned.1.call-update) | async-done | bytes 58720272 | tf_op jit(solution)/shard_map/all_gather | solution.py:328
  2476.6 27.6 %reduce_sum.602 = bf16[2048,3584]{1,0:T(8,128)(2,1)} reduce(bf16[4,2048,3584]{2,1,0:T(8,128)(2,1)} %bitcast.819, bf16[]{:T(256)} %constant.538.clone.1), dimensions={0}, to_apply=%region_74.75 | reduce | flops 22020096 | bytes 73400320 | tf_op jit(solution)/shard_map/reduce_sum | solution.py:328
  2504.2 10.4 slice.551
  2514.6 11.0 convert_element_type.724
  2525.7 12.6 copy.196
  2538.3 12.6 copy.202
  2550.9 11.8 slice_bitcast_fusion.1
  (860 shorter events, 777.6 us)
Async XLA Ops:
  7.2 36.5 %all-gather.49.cloned.1.call-start = ((), (), s32[]{:S(2)}) async-start(), calls=%async_computation.15 | async-start | bytes 1310720 | tf_op jit(solution)/shard_map/all_gather | solution.py:130
  10.3 1417.7 %copy-start.76 = (f32[1,2048]{1,0:T(1,128)}, f32[1,2048]{1,0:T(1,128)S(1)}, u32[]{:S(2)}) copy-start(f32[1,2048]{1,0:T(1,128)S(1)} %mul.1491) | copy-start | bytes 24580
  12.8 67.7 %all-gather.51.cloned.1.call-start = ((), (), s32[]{:S(2)}) async-start(), calls=%async_computation.16 | async-start | bytes 1310720 | tf_op jit(solution)/shard_map/all_gather | solution.py:146
  54.6 54.7 %all-gather.53.cloned.1.call-start = ((), (), s32[]{:S(2)}) async-start(), calls=%async_computation.17 | async-start | bytes 1310720 | tf_op jit(solution)/shard_map/all_gather | solution.py:147
  59.1 92.4 %reduce-scatter.16.cloned.1.call-start = ((), (), s32[]{:S(2)}) async-start(), calls=%async_computation.18 | async-start | bytes 1310720 | tf_op jit(solution)/shard_map/reduce_scatter | solution.py:173
  124.0 60.6 %all-gather.55.cloned.1.call-start = ((), (), s32[]{:S(2)}) async-start(), calls=%async_computation.19 | async-start | bytes 1310720 | tf_op jit(solution)/shard_map/all_gather | solution.py:130
  124.1 494.5 %copy-start.126 = (f32[1,2048]{1,0:T(1,128)}, f32[1,2048]{1,0:T(1,128)S(1)}, u32[]{:S(2)}) copy-start(f32[1,2048]{1,0:T(1,128)S(1)} %add.929) | copy-start | bytes 24580
  152.7 2.6 collective-permute-start
  156.7 72.6 %all-gather.57.cloned.1.call-start = ((), (), s32[]{:S(2)}) async-start(), calls=%async_computation.20 | async-start | bytes 1310720 | tf_op jit(solution)/shard_map/all_gather | solution.py:146
  203.4 54.1 %all-gather.59.cloned.1.call-start = ((), (), s32[]{:S(2)}) async-start(), calls=%async_computation.21 | async-start | bytes 1310720 | tf_op jit(solution)/shard_map/all_gather | solution.py:147
  210.9 90.9 %reduce-scatter.18.cloned.1.call-start = ((), (), s32[]{:S(2)}) async-start(), calls=%async_computation.22 | async-start | bytes 1310720 | tf_op jit(solution)/shard_map/reduce_scatter | solution.py:173
  274.3 61.5 %all-gather.61.cloned.1.call-start = ((), (), s32[]{:S(2)}) async-start(), calls=%async_computation.23 | async-start | bytes 1310720 | tf_op jit(solution)/shard_map/all_gather | solution.py:130
  303.6 2.8 collective-permute-start.1
  307.9 72.6 %all-gather.63.cloned.1.call-start = ((), (), s32[]{:S(2)}) async-start(), calls=%async_computation.24 | async-start | bytes 1310720 | tf_op jit(solution)/shard_map/all_gather | solution.py:146
  354.6 54.2 %all-gather.65.cloned.1.call-start = ((), (), s32[]{:S(2)}) async-start(), calls=%async_computation.25 | async-start | bytes 1310720 | tf_op jit(solution)/shard_map/all_gather | solution.py:147
  358.3 94.8 %reduce-scatter.20.cloned.1.call-start = ((), (), s32[]{:S(2)}) async-start(), calls=%async_computation.26 | async-start | bytes 1310720 | tf_op jit(solution)/shard_map/reduce_scatter | solution.py:173
  425.6 61.5 %all-gather.67.cloned.1.call-start = ((), (), s32[]{:S(2)}) async-start(), calls=%async_computation.27 | async-start | bytes 1310720 | tf_op jit(solution)/shard_map/all_gather | solution.py:130
  454.9 2.8 collective-permute-start.2
  459.2 72.4 %all-gather.69.cloned.1.call-start = ((), (), s32[]{:S(2)}) async-start(), calls=%async_computation.28 | async-start | bytes 1310720 | tf_op jit(solution)/shard_map/all_gather | solution.py:146
  505.7 54.0 %all-gather.71.cloned.1.call-start = ((), (), s32[]{:S(2)}) async-start(), calls=%async_computation.29 | async-start | bytes 1310720 | tf_op jit(solution)/shard_map/all_gather | solution.py:147
  509.4 79.7 %all-gather.99.cloned.1.call-start = ((), (), s32[]{:S(2)}) async-start(), calls=%async_computation.56 | async-start | bytes 1310720 | tf_op jit(solution)/shard_map/all_gather | solution.py:219
  511.8 106.8 %reduce-scatter.22.cloned.1.call-start = ((), (), s32[]{:S(2)}) async-start(), calls=%async_computation.30 | async-start | bytes 1310720 | tf_op jit(solution)/shard_map/reduce_scatter | solution.py:173
  576.6 76.0 %all-gather.73.cloned.1.call-start = ((), (), s32[]{:S(2)}) async-start(), calls=%async_computation.31 | async-start | bytes 1310720 | tf_op jit(solution)/shard_map/all_gather | solution.py:130
  619.7 4.2 collective-permute-start.3
  624.0 803.9 %copy-start.2 = (bf16[4,64,2048]{2,1,0:T(8,128)(2,1)}, bf16[4,64,2048]{2,1,0:T(8,128)(2,1)S(1)}, u32[]{:S(2)}) copy-start(bf16[4,64,2048]{2,1,0:T(8,128)(2,1)S(1)} %get-tuple-element.87) | copy-start | bytes 3145732
  625.6 85.8 %all-gather.75.cloned.1.call-start = ((), (), s32[]{:S(2)}) async-start(), calls=%async_computation.32 | async-start | bytes 1310720 | tf_op jit(solution)/shard_map/all_gather | solution.py:146
  671.4 54.0 %all-gather.77.cloned.1.call-start = ((), (), s32[]{:S(2)}) async-start(), calls=%async_computation.33 | async-start | bytes 1310720 | tf_op jit(solution)/shard_map/all_gather | solution.py:147
  685.3 68.3 %all-gather.97.cloned.1.call-start = ((), (), s32[]{:S(2)}) async-start(), calls=%async_computation.55 | async-start | bytes 1310720 | tf_op jit(solution)/shard_map/all_gather | solution.py:233
  697.8 84.0 %all-gather.101.cloned.1.call-start = ((), (), s32[]{:S(2)}) async-start(), calls=%async_computation.57 | async-start | bytes 1310720 | tf_op jit(solution)/shard_map/all_gather | solution.py:234
  709.2 117.6 %reduce-scatter.26.cloned.1.call-start = ((), (), s32[]{:S(2)}) async-start(), calls=%async_computation.35 | async-start | bytes 2621440 | tf_op jit(solution)/shard_map/reduce_scatter | solution.py:270
  791.5 88.6 %reduce-scatter.28.cloned.1.call-start = ((), (), s32[]{:S(2)}) async-start(), calls=%async_computation.36 | async-start | bytes 1310720 | tf_op jit(solution)/shard_map/reduce_scatter | solution.py:301
  852.6 54.2 %all-gather.103.cloned.1.call-start = ((), (), s32[]{:S(2)}) async-start(), calls=%async_computation.58 | async-start | bytes 1310720 | tf_op jit(solution)/shard_map/all_gather | solution.py:233
  853.2 208.8 %copy-start.160 = (f32[64]{0:T(128)}, f32[64]{0:T(128)S(1)}, u32[]{:S(2)}) copy-start(f32[64]{0:T(128)S(1)} %broadcast_multiply_fusion.2) | copy-start | bytes 772
  853.4 82.9 %all-gather.79.cloned.1.call-start = ((), (), s32[]{:S(2)}) async-start(), calls=%async_computation.37 | async-start | bytes 1310720 | tf_op jit(solution)/shard_map/all_gather | solution.py:219
  885.6 3.4 collective-permute-start.4
  891.3 72.4 %all-gather.105.cloned.1.call-start = ((), (), s32[]{:S(2)}) async-start(), calls=%async_computation.59 | async-start | bytes 1310720 | tf_op jit(solution)/shard_map/all_gather | solution.py:234
  891.9 116.8 %reduce-scatter.30.cloned.1.call-start = ((), (), s32[]{:S(2)}) async-start(), calls=%async_computation.38 | async-start | bytes 2621440 | tf_op jit(solution)/shard_map/reduce_scatter | solution.py:270
  973.4 88.7 %reduce-scatter.32.cloned.1.call-start = ((), (), s32[]{:S(2)}) async-start(), calls=%async_computation.39 | async-start | bytes 1310720 | tf_op jit(solution)/shard_map/reduce_scatter | solution.py:301
  1034.6 54.0 %all-gather.107.cloned.1.call-start = ((), (), s32[]{:S(2)}) async-start(), calls=%async_computation.60 | async-start | bytes 1310720 | tf_op jit(solution)/shard_map/all_gather | solution.py:233
  1035.2 83.0 %all-gather.81.cloned.1.call-start = ((), (), s32[]{:S(2)}) async-start(), calls=%async_computation.40 | async-start | bytes 1310720 | tf_op jit(solution)/shard_map/all_gather | solution.py:219
  1067.5 3.4 collective-permute-start.5
  1073.2 72.6 %all-gather.109.cloned.1.call-start = ((), (), s32[]{:S(2)}) async-start(), calls=%async_computation.61 | async-start | bytes 1310720 | tf_op jit(solution)/shard_map/all_gather | solution.py:234
  1074.0 116.8 %reduce-scatter.34.cloned.1.call-start = ((), (), s32[]{:S(2)}) async-start(), calls=%async_computation.41 | async-start | bytes 2621440 | tf_op jit(solution)/shard_map/reduce_scatter | solution.py:270
  1155.5 88.7 %reduce-scatter.36.cloned.1.call-start = ((), (), s32[]{:S(2)}) async-start(), calls=%async_computation.42 | async-start | bytes 1310720 | tf_op jit(solution)/shard_map/reduce_scatter | solution.py:301
  1216.7 54.2 %all-gather.111.cloned.1.call-start = ((), (), s32[]{:S(2)}) async-start(), calls=%async_computation.62 | async-start | bytes 1310720 | tf_op jit(solution)/shard_map/all_gather | solution.py:233
  1217.4 82.9 %all-gather.83.cloned.1.call-start = ((), (), s32[]{:S(2)}) async-start(), calls=%async_computation.43 | async-start | bytes 1310720 | tf_op jit(solution)/shard_map/all_gather | solution.py:219
  1248.1 3.4 collective-permute-start.6
  1253.9 73.9 %all-gather.113.cloned.1.call-start = ((), (), s32[]{:S(2)}) async-start(), calls=%async_computation.63 | async-start | bytes 1310720 | tf_op jit(solution)/shard_map/all_gather | solution.py:234
  1254.5 118.3 %reduce-scatter.38.cloned.1.call-start = ((), (), s32[]{:S(2)}) async-start(), calls=%async_computation.44 | async-start | bytes 2621440 | tf_op jit(solution)/shard_map/reduce_scatter | solution.py:270
  1337.4 88.6 %reduce-scatter.40.cloned.1.call-start = ((), (), s32[]{:S(2)}) async-start(), calls=%async_computation.45 | async-start | bytes 1310720 | tf_op jit(solution)/shard_map/reduce_scatter | solution.py:301
  1398.6 54.2 %all-gather.115.cloned.1.call-start = ((), (), s32[]{:S(2)}) async-start(), calls=%async_computation.64 | async-start | bytes 1310720 | tf_op jit(solution)/shard_map/all_gather | solution.py:233
  1399.4 83.0 %all-gather.85.cloned.1.call-start = ((), (), s32[]{:S(2)}) async-start(), calls=%async_computation.46 | async-start | bytes 1310720 | tf_op jit(solution)/shard_map/all_gather | solution.py:219
  1430.1 3.4 collective-permute-start.7
  1435.9 74.2 %all-gather.117.cloned.1.call-start = ((), (), s32[]{:S(2)}) async-start(), calls=%async_computation.65 | async-start | bytes 1310720 | tf_op jit(solution)/shard_map/all_gather | solution.py:234
  1436.6 165.5 %reduce-scatter.42.cloned.1.call-start = ((), (), s32[]{:S(2)}) async-start(), calls=%async_computation.47 | async-start | bytes 2621440 | tf_op jit(solution)/shard_map/reduce_scatter | solution.py:270
  1519.4 124.9 %all-gather.89.cloned.1.call-start = ((), (), s32[]{:S(2)}) async-start(), calls=%async_computation.50 | async-start | bytes 1310720 | tf_op jit(solution)/shard_map/all_gather | solution.py:296
  1520.1 140.1 %all-gather.87.cloned.1.call-start = ((), (), s32[]{:S(2)}) async-start(), calls=%async_computation.49 | async-start | bytes 1310720 | tf_op jit(solution)/shard_map/all_gather | solution.py:296
  1520.7 154.6 %all-gather.91.cloned.1.call-start = ((), (), s32[]{:S(2)}) async-start(), calls=%async_computation.51 | async-start | bytes 1310720 | tf_op jit(solution)/shard_map/all_gather | solution.py:296
  1521.3 169.6 %all-gather.93.cloned.1.call-start = ((), (), s32[]{:S(2)}) async-start(), calls=%async_computation.52 | async-start | bytes 1310720 | tf_op jit(solution)/shard_map/all_gather | solution.py:296
  1531.7 175.0 %all-gather.95.cloned.1.call-start = ((), (), s32[]{:S(2)}) async-start(), calls=%async_computation.53 | async-start | bytes 1310720 | tf_op jit(solution)/shard_map/all_gather | solution.py:296
  1541.0 203.2 %reduce-scatter.24.cloned.1.call-start = ((), (), s32[]{:S(2)}) async-start(), calls=%async_computation.34 | async-start | bytes 1310720 | tf_op jit(solution)/shard_map/reduce_scatter | solution.py:173
  1553.7 203.3 %reduce-scatter.44.cloned.1.call-start = ((), (), s32[]{:S(2)}) async-start(), calls=%async_computation.48 | async-start | bytes 1310720 | tf_op jit(solution)/shard_map/reduce_scatter | solution.py:301
  1617.6 349.0 %all-reduce.4.cloned.1.call-start = ((), (), s32[]{:S(2)}) async-start(), calls=%async_computation.54 | async-start | bytes 20971520 | tf_op jit(solution)/shard_map/psum | solution.py:329
  1643.8 832.7 %all-gather.119.cloned.1.call-start = ((), (), s32[]{:S(2)}) async-start(), calls=%async_computation.66 | async-start | bytes 73400320 | tf_op jit(solution)/shard_map/all_gather | solution.py:328
  (169 other events, 1960.6 us)
Sparse Core Ops, SparseCore 0:
  13.0 30.6 all-gather.48
  54.7 25.7 all-gather.50
  82.9 26.3 all-gather.52
  124.1 27.2 reduce-scatter.15
  156.8 27.7 all-gather.54
  203.5 25.7 all-gather.56
  231.1 26.3 all-gather.58
  274.4 27.2 reduce-scatter.17
  308.0 27.7 all-gather.60
  354.8 25.7 all-gather.62
  382.4 26.3 all-gather.64
  425.8 27.2 reduce-scatter.19
  459.3 27.7 all-gather.66
  505.9 25.7 all-gather.68
  533.3 26.3 all-gather.70
  561.1 27.9 all-gather.98
  591.8 26.6 reduce-scatter.21
  625.7 26.8 all-gather.72
  671.5 25.7 all-gather.74
  699.0 26.3 all-gather.76
  727.2 26.3 all-gather.96
  755.4 26.3 all-gather.100
  791.6 35.1 reduce-scatter.25
  852.8 27.2 reduce-scatter.27
  881.9 24.8 all-gather.102
  908.2 27.9 all-gather.78
  937.9 25.7 all-gather.104
  973.5 35.1 reduce-scatter.29
  1034.7 27.2 reduce-scatter.31
  1063.7 24.8 all-gather.106
  1090.2 27.9 all-gather.80
  1120.0 25.7 all-gather.108
  1155.6 35.1 reduce-scatter.33
  1216.8 27.3 reduce-scatter.35
  1246.0 24.8 all-gather.110
  1272.3 27.9 all-gather.82
  1302.0 25.7 all-gather.112
  1337.6 35.1 reduce-scatter.37
  1398.8 27.2 reduce-scatter.39
  1427.9 24.8 all-gather.114
  1454.4 27.9 all-gather.84
  1484.2 25.7 all-gather.116
  1519.5 35.1 reduce-scatter.41
  1556.3 27.9 all-gather.88
  1585.7 27.3 all-gather.86
  1614.5 27.3 all-gather.90
  1643.4 27.3 all-gather.92
  1672.2 27.3 all-gather.94
  1701.7 26.6 reduce-scatter.23
  1731.3 25.7 reduce-scatter.43
  1761.0 205.5 all-reduce.3
  1969.0 507.4 all-gather.118
